TPU v7x, 128 devices: a whole 4x4x4 slice. The times are simulated.
128 devices in a mesh: aux: 16 (over z, x_lo, core), rows: 8 (over y, x_hi).
Axes of the slice: x: 4 (x_hi: 2, x_lo: 2; x = x_hi * 2 + x_lo), y: 4, z: 4, core: 2. Of those that a mesh axis runs over, the one named last changes fastest.
Arguments:
- three_center: bfloat16 [128, 40, 16, 128, 128], P('aux', 'rows'), may hold values from -6 to 6
- coeffs: bfloat16 [16384, 128], P('aux'), may hold values from -0.01171875 to 0.01171875
- sig_blocks: int32 [40, 16], P('rows'), may hold values from 0 to 7
- k_columns: int32 [40, 12], P('rows'), may hold values from 0 to 39, as said below
- owners: int32 [480, 1], P('rows'), may hold values from 0 to 7; in each aligned block of 60 rows (0 to 59, 60 to 119, ...) at most 15 rows name the same one
Outputs:
- exchange_blocks: float32 [960, 128, 128], P('rows', 'aux')
Inputs may be any that keep to these rules, and one draw needn't show every extreme that they name: `owners`: among the 60 entries of one rows index, no owner is named more than 15 times. `k_columns`: the 12 entries of one row block are distinct, and the first entry of row block m is m itself.
All inputs are finite; a program needn't handle non-finite values.
Results may differ from a plain program's by a relative error of at most 0.0014.
Values may be sent and summed in bfloat16 or wider, within the bound.
A program may use at most 128 MiB of HBM per device.

v0:
```python
import jax
import jax.numpy as jnp
from jax import lax
from jax.sharding import PartitionSpec as P

BS = 128
OCC = 128
BLK_DEV = 8
CAP = 15


def bucket(values, owner_ids, owner_total, capacity):
    onehot = (owner_ids[:, None] == jnp.arange(owner_total, dtype=jnp.int32)[None, :]).astype(
        jnp.int32
    )
    ranks = jnp.sum(jnp.cumsum(onehot, axis=0) * onehot, axis=1) - 1
    target = owner_ids * capacity + ranks
    buffer = jnp.zeros((owner_total * capacity,) + values.shape[1:], values.dtype)
    return buffer.at[target].set(values)


def per_device(three_center, coeffs, sig_blocks, k_columns, owners):
    row_local = three_center.shape[1]
    owner_count = three_center.shape[2]
    panels = lax.all_gather(coeffs, "aux", axis=0, tiled=True)
    blocks = panels.reshape(owner_count * BLK_DEV, BS, OCC)
    wanted = sig_blocks + (jnp.arange(owner_count, dtype=jnp.int32) * BLK_DEV)[None, :]
    picked = blocks[wanted]
    half_sum = jnp.einsum(
        "pmqab,mqbo->pmao", three_center, picked, preferred_element_type=jnp.float32
    )
    half = half_sum.astype(jnp.bfloat16)
    every_row = lax.all_gather(half, "rows", axis=1, tiled=True)
    pieces_list = []
    for index in range(row_local):
        partners = jnp.take(every_row, k_columns[index], axis=1)
        pieces_list.append(
            jnp.einsum(
                "pai,psbi->sab", half[:, index], partners, preferred_element_type=jnp.float32
            )
        )
    partial_value = jnp.concatenate(pieces_list, axis=0)
    owner_total = lax.axis_size("rows")
    owner_ids = owners[:, 0]
    reduced = lax.psum_scatter(partial_value, "aux", scatter_dimension=1, tiled=True)
    buffer = bucket(reduced, owner_ids, owner_total, CAP)
    buffer = buffer.reshape(owner_total, CAP, reduced.shape[1], BS)
    arrived = lax.all_to_all(buffer, "rows", split_axis=0, concat_axis=0, tiled=True)
    return arrived.reshape(owner_total * CAP, reduced.shape[1], BS)


def solution(mesh):
    return jax.shard_map(
        per_device,
        mesh=mesh,
        in_specs=(
            P("aux", "rows", None, None, None),
            P("aux", None),
            P("rows", None),
            P("rows", None),
            P("rows", None),
        ),
        out_specs=P("rows", "aux", None),
        check_vma=False,
    )
```

profile of v0, /device:TPU:0, one launch (start us, length us, event | category | flops | bytes accessed | tf_op | source)
XLA Modules:
  0.0 333.1 jit_solution(17910618142357279781)
XLA Ops:
  6.5 0.0 all-gather.3.cloned.1.call-start
  6.5 0.7 all-gather.3.cloned.1.call-update
  7.3 0.0 all-gather.5.cloned.1.call-start
  7.3 0.7 compare_select_fusion
  8.0 0.1 reshape.72
  8.1 40.8 %all-gather.3.cloned.1.call-done = bf16[16384,128]{1,0:T(8,128)(2,1)} async-done(((bf16[1024,128]{1,0:T(8,128)(2,1)}), bf16[16384,128]{1,0:T(8,128)(2,1)}) %all-gather.3.cloned.1.call-update) | async-done | bytes 4194320 | tf_op jit(solution)/shard_map/all_gather | solution.py:25
  48.9 3.2 gather_fusion
  52.1 12.0 %fusion.29 = bf16[8,5,128,128]{2,3,0,1:T(8,128)(2,1)} fusion(bf16[5,16,128,128,1]{3,2,1,4,0:T(8,128)(2,1)S(1)} %bitcast.135, bf16[8,5,16,128,128]{4,3,2,1,0:T(8,128)(2,1)} %param.7), kind=kOutput, calls=%fused_computation.35 | convolution fusion | flops 2685009920 | bytes 24903680 | tf_op jit(solution)/shard_map/pmqab,mqbo->pmao/dot_general | solution.py:29
  64.1 0.0 copy-start.1
  64.1 2.4 copy.33
  66.6 0.0 all-gather.5.cloned.1.call-update
  66.6 0.0 reduce-scatter.2.cloned.1.call-start
  66.7 0.0 copy-done.1
  66.7 125.3 %all-gather.5.cloned.1.call-done = bf16[8,40,128,128]{3,2,0,1:T(8,128)(2,1)} async-done(((bf16[8,5,128,128]{3,2,0,1:T(8,128)(2,1)}), bf16[8,40,128,128]{3,2,0,1:T(8,128)(2,1)}) %all-gather.5.cloned.1.call-update) | async-done | bytes 10485776 | tf_op jit(solution)/shard_map/all_gather | solution.py:33
  192.0 5.1 %gather_fusion.1 = bf16[12,8,128,128]{3,2,1,0:T(8,128)(2,1)S(1)} fusion(bf16[8,40,128,128]{3,2,0,1:T(8,128)(2,1)} %all-gather.5.cloned.1.call-done, s32[1024]{0:T(1024)S(1)} %pad_clamp_fusion.4), kind=kCustom, calls=%fused_computation.clone | custom fusion | bytes 6291504 | tf_op jit(solution)/shard_map/jit(_take)/gather | solution.py:36
  197.2 2.9 fusion.35
  200.0 5.1 %gather_fusion.2 = bf16[12,8,128,128]{3,2,1,0:T(8,128)(2,1)S(1)} fusion(bf16[8,40,128,128]{3,2,0,1:T(8,128)(2,1)} %all-gather.5.cloned.1.call-done, s32[1024]{0:T(1024)S(1)} %get-tuple-element.27), kind=kCustom, calls=%fused_computation.1.clone | custom fusion | bytes 6291504 | tf_op jit(solution)/shard_map/jit(_take)/gather | solution.py:36
  205.2 2.8 fusion.41
  208.0 5.1 %gather_fusion.3 = bf16[12,8,128,128]{3,2,1,0:T(8,128)(2,1)S(1)} fusion(bf16[8,40,128,128]{3,2,0,1:T(8,128)(2,1)} %all-gather.5.cloned.1.call-done, s32[1024]{0:T(1024)S(1)} %get-tuple-element.26), kind=kCustom, calls=%fused_computation.2.clone | custom fusion | bytes 6291504 | tf_op jit(solution)/shard_map/jit(_take)/gather | solution.py:36
  213.1 2.9 fusion.47
  216.0 5.1 %gather_fusion.4 = bf16[12,8,128,128]{3,2,1,0:T(8,128)(2,1)S(1)} fusion(bf16[8,40,128,128]{3,2,0,1:T(8,128)(2,1)} %all-gather.5.cloned.1.call-done, s32[1024]{0:T(1024)S(1)} %get-tuple-element.25), kind=kCustom, calls=%fused_computation.3.clone | custom fusion | bytes 6291504 | tf_op jit(solution)/shard_map/jit(_take)/gather | solution.py:36
  221.1 2.9 fusion.53
  224.1 5.1 %gather_fusion.5 = bf16[12,8,128,128]{3,2,1,0:T(8,128)(2,1)S(1)} fusion(bf16[8,40,128,128]{3,2,0,1:T(8,128)(2,1)} %all-gather.5.cloned.1.call-done, s32[1024]{0:T(1024)S(1)} %get-tuple-element.24), kind=kCustom, calls=%fused_computation.4.clone | custom fusion | bytes 6291504 | tf_op jit(solution)/shard_map/jit(_take)/gather | solution.py:36
  229.2 2.9 fusion.59
  232.1 5.1 %copy.39 = f32[60,128,128]{2,0,1:T(8,128)} copy(f32[60,128,128]{1,2,0:T(8,128)} %fusion.59) | data formatting | bytes 7864320 | tf_op jit(solution)/shard_map/concatenate | solution.py:42
  237.2 0.0 copy-start
  237.2 0.0 reduce-scatter.2.cloned.1.call-update
  237.2 0.6 copy-done
  237.8 0.1 fusion.62
  237.9 0.1 reduce_window_sum.11
  238.0 0.2 select_reduce_fusion
  238.2 67.7 %reduce-scatter.2.cloned.1.call-done = f32[60,8,128]{2,0,1:T(8,128)} async-done(((f32[60,128,128]{2,0,1:T(8,128)}), f32[60,8,128]{2,0,1:T(8,128)}) %reduce-scatter.2.cloned.1.call-update) | async-done | bytes 245776 | tf_op jit(solution)/shard_map/reduce_scatter | solution.py:45
  305.9 1.1 copy.40
  307.1 2.5 scatter_fusion
  309.6 16.2 %all_to_all.5 = f32[8,15,8,128]{3,2,1,0:T(8,128)S(1)} all-to-all(f32[8,15,8,128]{3,2,1,0:T(8,128)S(1)} %bitcast.134), channel_id=1, replica_groups=mesh['aux'=16,'rows'=8] {'rows'}, dimensions={0} | all-to-all | bytes 983040 | tf_op jit(solution)/shard_map/all_to_all | solution.py:48
  325.8 0.8 copy.70
  (8 shorter events, 0.1 us)
Async XLA Ops:
  6.5 42.4 %all-gather.3.cloned.1.call-start = ((), (), s32[]{:S(2)}) async-start(), calls=%async_computation.2 | async-start | bytes 4456448 | tf_op jit(solution)/shard_map/all_gather | solution.py:25
  7.3 184.8 %all-gather.5.cloned.1.call-start = ((), (), s32[]{:S(2)}) async-start(), calls=%async_computation.3 | async-start | bytes 11796480 | tf_op jit(solution)/shard_map/all_gather | solution.py:33
  64.1 2.5 copy-start.1
  66.6 239.3 %reduce-scatter.2.cloned.1.call-start = ((), (), s32[]{:S(2)}) async-start(), calls=%async_computation.4 | async-start | bytes 4456448 | tf_op jit(solution)/shard_map/reduce_scatter | solution.py:45
  237.2 0.7 copy-start
Sparse Core Ops, SparseCore 0:
  9.0 39.8 all-gather.2
  66.7 125.2 all-gather.4
  237.3 68.5 reduce-scatter.1
where the time goes:
time: 334 us; the launch traced here: 333 us
  waiting for transfers between devices  235 us (70%)
  local copies, waits for them, and re-layouts  41.5 us (12%)
  matrix products  26.4 us (8%)
  blocking collectives  16.2 us (5%)
  between operations  13.2 us (4%)
    all_gather x1, waiting for transfers between devices, per_device(): every_row = lax.all_gather(half, 'rows', axis=1, tiled=True)  125 us
    reduce_scatter x1, waiting for transfers between devices, per_device(): lax.psum_scatter(partial_value, 'aux', scatter_dimension=1, tiled=True)  67.7 us
    all_gather x1, waiting for transfers between devices, per_device(): panels = lax.all_gather(coeffs, 'aux', axis=0, tiled=True)  40.8 us
    gather x5, local copies, waits for them, and re-layouts, per_device(): partners = jnp.take(every_row, k_columns[index], axis=1)  25.6 us
    all_to_all x1, blocking collectives, per_device(): lax.all_to_all(buffer, 'rows', split_axis=0, concat_axis=0, tiled=True)  16.2 us
    dot_general x5, matrix products, per_device(): jnp.einsum('pai,psbi->sab', half[:, index], partners, preferred_element_t...  14.4 us
    dot_general x1, matrix products, per_device(): jnp.einsum('pmqab,mqbo->pmao', three_center, picked, preferred_element_ty...  12 us
  transfers between devices with their start and end apart: 3, of which 3 were waited for; matrix products, arithmetic and copies ran while one was open for 0% of the time, Pallas kernels for 0%

commit v1 on v0

v1 whole, which is shorter than its diff:
```python
import jax
import jax.numpy as jnp
from jax import lax
from jax.experimental import pallas as pl
from jax.experimental.pallas import tpu as pltpu
from jax.sharding import PartitionSpec as P

BS = 128
OCC = 128
BLK_DEV = 8
RB = 5
KS = 12
CAP = 15
F32 = jnp.float32
BF16 = jnp.bfloat16


def remote(src, dst, send_sem, recv_sem, device):
    return pltpu.make_async_remote_copy(
        src_ref=src,
        dst_ref=dst,
        send_sem=send_sem,
        recv_sem=recv_sem,
        device_id=device,
        device_id_type=pl.DeviceIdType.MESH,
    )


def kernel(
    t_hbm,
    coeff_ref,
    sig_ref,
    cols_ref,
    slot_ref,
    out_ref,
    t_v,
    picks,
    h_all,
    cols_mine,
    cols_got,
    cols_sm,
    part,
    core_in,
    r1a,
    r1b,
    r2a,
    r2b,
    red,
    abuf,
    t_sem,
    p_send,
    p_recv,
    b_send,
    b_recv,
    x_send,
    x_recv,
    k_sem,
    y_send,
    y_recv,
    c_send,
    c_recv,
    r_send,
    r_recv,
    a_send,
    a_recv,
):
    aux = lax.axis_index("aux")
    rows = lax.axis_index("rows")
    z, xl, c = aux // 4, (aux // 2) % 2, aux % 2
    y, xh = rows // 2, rows % 2
    x = xh * 2 + xl
    zx = aux // 2

    def chip(px, py, pz, core):
        return {"aux": pz * 4 + (px % 2) * 2 + core, "rows": py * 2 + px // 2}

    sibling = {"aux": zx * 2 + 1 - c, "rows": rows}
    partner = {"aux": aux, "rows": y * 2 + 1 - xh}
    y_right, y_left = chip(x, (y + 1) % 4, z, c), chip(x, (y + 3) % 4, z, c)
    same = [{"aux": ((zx + e) % 8) * 2 + c, "rows": rows} for e in range(1, 8)]
    owners = [{"aux": aux, "rows": (rows + d) % 8} for d in range(1, 8)]
    across = {"aux": z * 4 + (1 - xl) * 2 + c, "rows": y * 2 + 1 - xh}

    loads = []
    for m in range(RB):
        load = pltpu.make_async_copy(t_hbm.at[:, m], t_v.at[m], t_sem.at[m])
        load.start()
        loads.append(load)

    barrier = pltpu.get_barrier_semaphore()
    greeted = same + [sibling] + owners + [across]
    for device in greeted:
        pl.semaphore_signal(barrier, inc=1, device_id=device, device_id_type=pl.DeviceIdType.MESH)

    for m in range(RB):
        picks[m, zx, c] = coeff_ref[sig_ref[m, aux]]
    lane = lax.broadcasted_iota(jnp.int32, (8, 128), 1)
    mine = jnp.zeros((8, 128), jnp.int32)
    for m in range(RB):
        for s in range(KS):
            mine = jnp.where(lane == m * KS + s, cols_ref[m, s], mine)
    cols_mine[...] = mine
    pl.semaphore_wait(barrier, len(greeted))

    sends = []

    def send(*args):
        copy = remote(*args)
        copy.start()
        sends.append(copy)

    for m in range(RB):
        block = picks.at[m, zx, c]
        for e in range(7):
            send(block, block, p_send.at[m, e], p_recv.at[m, e], same[e])
    send(cols_mine, cols_got, k_sem.at[0], k_sem.at[1], partner)

    def row_block(py, which, m):
        owner = xh if which == 0 else 1 - xh
        return h_all.at[(py * 2 + owner) * RB + m]

    def pass_on(m, which):
        block = row_block(y, which, m)
        send(block, block, y_send.at[m, which], y_recv.at[m, which], y_right)
        send(block, block, y_send.at[m, 2 + which], y_recv.at[m, 2 + which], y_left)

    def relay(m, which):
        if which == 0:
            block = row_block((y + 3) % 4, 0, m)
            remote(block, block, y_send.at[m, 0], y_recv.at[m, 0], y_left).wait_recv()
            send(block, block, y_send.at[m, 4], y_recv.at[m, 4], y_right)
        else:
            block = row_block((y + 1) % 4, 1, m)
            remote(block, block, y_send.at[m, 3], y_recv.at[m, 3], y_right).wait_recv()
            send(block, block, y_send.at[m, 5], y_recv.at[m, 5], y_left)

    def from_partner(m):
        block = row_block(y, 1, m)
        remote(block, block, x_send.at[m], x_recv.at[m], partner).wait_recv()
        pass_on(m, 1)

    for m in range(RB):
        for e in range(7):
            block = picks.at[m, (zx + 7 - e) % 8, c]
            remote(block, block, p_send.at[m, e], p_recv.at[m, e], same[e]).wait_recv()
        block = picks.at[m, :, c]
        send(block, block, b_send.at[m], b_recv.at[m], sibling)
        other = picks.at[m, :, 1 - c]
        remote(other, other, b_send.at[m], b_recv.at[m], sibling).wait_recv()
        loads[m].wait()

        def half(g, carry, m=m):
            chosen = (1 - g) * (1 - xh) + g * xh
            slab = jnp.concatenate(
                [t_v[m, pl.ds(chosen * 4, 4), q].reshape(4 * BS, BS) for q in range(16)], axis=1
            )
            weight = picks[m].reshape(16 * BS, OCC)
            value = jnp.dot(slab, weight, preferred_element_type=F32).astype(BF16)
            where = (1 - g) * (8 * RB + m) + g * (rows * RB + m)
            for p in range(4):
                h_all[where, :, p * OCC : (p + 1) * OCC] = value[p * BS : (p + 1) * BS]
            return carry

        lax.fori_loop(0, 2, half, 0)
        send(
            h_all.at[8 * RB + m],
            h_all.at[rows * RB + m],
            x_send.at[m],
            x_recv.at[m],
            partner,
        )
        pass_on(m, 0)
        if m >= 1:
            from_partner(m - 1)
        if m >= 2:
            relay(m - 2, 0)
    from_partner(RB - 1)
    for m in range(RB):
        if m >= RB - 2:
            relay(m, 0)
        relay(m, 1)

    remote(cols_mine, cols_got, k_sem.at[0], k_sem.at[1], partner).wait_recv()
    inward = pltpu.make_async_copy(cols_got, cols_sm, k_sem.at[2])
    inward.start()
    inward.wait()
    for m in range(RB):
        block = row_block((y + 3) % 4, 1, m)
        remote(block, block, y_send.at[m, 1], y_recv.at[m, 1], y_left).wait_recv()
        block = row_block((y + 1) % 4, 0, m)
        remote(block, block, y_send.at[m, 2], y_recv.at[m, 2], y_right).wait_recv()
        block = row_block((y + 2) % 4, 0, m)
        remote(block, block, y_send.at[m, 4], y_recv.at[m, 4], y_left).wait_recv()
        block = row_block((y + 2) % 4, 1, m)
        remote(block, block, y_send.at[m, 5], y_recv.at[m, 5], y_right).wait_recv()

    u = (1 - c) * x + c * z
    v = (1 - c) * z + c * x
    right1 = chip((x + 1 - c) % 4, y, (z + c) % 4, c)
    left1 = chip((x + 3 * (1 - c)) % 4, y, (z + 3 * c) % 4, c)
    right2 = chip((x + c) % 4, y, (z + 1 - c) % 4, c)
    left2 = chip((x + 3 * c) % 4, y, (z + 3 * (1 - c)) % 4, c)
    u_next, u_last, u_far = (u + 1) % 4, (u + 3) % 4, (u + 2) % 4
    v_next, v_last, v_far = (v + 1) % 4, (v + 3) % 4, (v + 2) % 4

    def products(m):
        def pair(i, carry):
            g, sp = i // (KS // 2), i % (KS // 2)
            left = h_all[(y * 2 + g) * RB + m]
            cols = [
                jnp.where(g == xh, cols_ref[m, sp * 2 + h], cols_sm[0, m * KS + sp * 2 + h])
                for h in range(2)
            ]
            right = jnp.concatenate([h_all[cols[0]], h_all[cols[1]]], axis=0)
            value = lax.dot_general(
                left, right, (((1,), (1,)), ((), ())), preferred_element_type=F32
            )
            for j in range(16):
                jz, jx, jc = j // 4, (j // 2) % 2, j % 2
                jx = g * 2 + jx
                ju, jv = (jx, jz) if jc == 0 else (jz, jx)
                for h in range(2):
                    part[m, jc, ju, jv, sp * 2 + h] = value[
                        j * 8 : j * 8 + 8, h * BS : (h + 1) * BS
                    ]
            return carry

        lax.fori_loop(0, KS, pair, 0)
        send(part.at[m, 1 - c], core_in.at[m], c_send.at[m], c_recv.at[m], sibling)

    def stage1(m):
        remote(core_in.at[m], core_in.at[m], c_send.at[m], c_recv.at[m], sibling).wait_recv()

        def add(i, carry):
            part[m, c, i] = part[m, c, i] + core_in[m, i]
            return carry

        lax.fori_loop(0, 4, add, 0)
        far = part.at[m, c, u_far]
        send(far.at[0:2], r1a.at[m, 0], r_send.at[m, 0], r_recv.at[m, 0], right1)
        send(far.at[2:4], r1a.at[m, 1], r_send.at[m, 1], r_recv.at[m, 1], left1)

    def arrive(buffer, m, i, device):
        remote(buffer, buffer, r_send.at[m, i], r_recv.at[m, i], device).wait_recv()

    def stage2(m):
        arrive(r1a.at[m, 0], m, 0, left1)
        part[m, c, u_next, 0:2] = part[m, c, u_next, 0:2] + r1a[m, 0]
        send(part.at[m, c, u_next], r1b.at[m, 0], r_send.at[m, 2], r_recv.at[m, 2], right1)
        arrive(r1a.at[m, 1], m, 1, right1)
        part[m, c, u_last, 2:4] = part[m, c, u_last, 2:4] + r1a[m, 1]
        send(part.at[m, c, u_last], r1b.at[m, 1], r_send.at[m, 3], r_recv.at[m, 3], left1)

    def stage3(m):
        arrive(r1b.at[m, 0], m, 2, left1)
        arrive(r1b.at[m, 1], m, 3, right1)
        part[m, c, u] = part[m, c, u] + r1b[m, 0] + r1b[m, 1]
        far = part.at[m, c, u, v_far]
        send(far.at[0:6], r2a.at[m, 0], r_send.at[m, 4], r_recv.at[m, 4], right2)
        send(far.at[6:12], r2a.at[m, 1], r_send.at[m, 5], r_recv.at[m, 5], left2)

    def stage4(m):
        arrive(r2a.at[m, 0], m, 4, left2)
        part[m, c, u, v_next, 0:6] = part[m, c, u, v_next, 0:6] + r2a[m, 0]
        send(part.at[m, c, u, v_next], r2b.at[m, 0], r_send.at[m, 6], r_recv.at[m, 6], right2)
        arrive(r2a.at[m, 1], m, 5, right2)
        part[m, c, u, v_last, 6:12] = part[m, c, u, v_last, 6:12] + r2a[m, 1]
        send(part.at[m, c, u, v_last], r2b.at[m, 1], r_send.at[m, 7], r_recv.at[m, 7], left2)

    def stage5(m):
        arrive(r2b.at[m, 0], m, 6, left2)
        arrive(r2b.at[m, 1], m, 7, right2)
        red[1 + m * KS : 1 + (m + 1) * KS] = part[m, c, u, v] + r2b[m, 0] + r2b[m, 1]

    red[0] = jnp.zeros((8, BS), F32)
    stages = [products, stage1, stage2, stage3, stage4, stage5]
    for t in range(RB + 5):
        for lag, stage in enumerate(stages):
            if 0 <= t - lag < RB:
                stage(t - lag)

    for d in range(7):
        owner = (rows + d + 1) % 8
        for s in range(CAP):
            abuf[d, s] = red[slot_ref[owner, s]]
        send(
            abuf.at[d],
            out_ref.at[pl.ds(rows * CAP, CAP)],
            a_send.at[d],
            a_recv.at[d],
            owners[d],
        )
    for s in range(CAP):
        out_ref[rows * CAP + s] = red[slot_ref[rows, s]]
    for d in range(7):
        landed = out_ref.at[pl.ds(((rows + 7 - d) % 8) * CAP, CAP)]
        remote(abuf.at[d], landed, a_send.at[d], a_recv.at[d], owners[d]).wait_recv()
    for copy in sends:
        copy.wait_send()


def slots_of(owner_ids, total):
    count = owner_ids.shape[0]
    at = jnp.arange(count, dtype=jnp.int32)
    same = (owner_ids[:, None] == owner_ids[None, :]) & (at[None, :] < at[:, None])
    target = owner_ids * CAP + jnp.sum(same.astype(jnp.int32), axis=1)
    place = jnp.arange(total * CAP, dtype=jnp.int32)
    hit = target[None, :] == place[:, None]
    return jnp.sum(jnp.where(hit, at[None, :] + 1, 0), axis=1).reshape(total, CAP)


def per_device(three_center, coeffs, sig_blocks, k_columns, owners):
    slots = slots_of(owners[:, 0], 8)
    vmem, smem = pltpu.VMEM, pltpu.SMEM
    dma = pltpu.SemaphoreType.DMA
    return pl.pallas_call(
        kernel,
        out_shape=jax.ShapeDtypeStruct((8 * CAP, 8, BS), F32),
        in_specs=[
            pl.BlockSpec(memory_space=pl.ANY),
            pl.BlockSpec(memory_space=vmem),
            pl.BlockSpec(memory_space=smem),
            pl.BlockSpec(memory_space=smem),
            pl.BlockSpec(memory_space=smem),
        ],
        out_specs=pl.BlockSpec(memory_space=vmem),
        scratch_shapes=[
            vmem((RB, 8, 16, BS, BS), BF16),
            vmem((RB, 8, 2, BS, OCC), BF16),
            vmem((9 * RB, BS, 4 * OCC), BF16),
            vmem((8, 128), jnp.int32),
            vmem((8, 128), jnp.int32),
            smem((8, 128), jnp.int32),
            vmem((RB, 2, 4, 4, KS, 8, BS), F32),
            vmem((RB, 4, 4, KS, 8, BS), F32),
            vmem((RB, 2, 2, KS, 8, BS), F32),
            vmem((RB, 2, 4, KS, 8, BS), F32),
            vmem((RB, 2, KS // 2, 8, BS), F32),
            vmem((RB, 2, KS, 8, BS), F32),
            vmem((1 + RB * KS, 8, BS), F32),
            vmem((7, CAP, 8, BS), F32),
            dma((RB,)),
            dma((RB, 7)),
            dma((RB, 7)),
            dma((RB,)),
            dma((RB,)),
            dma((RB,)),
            dma((RB,)),
            dma((3,)),
            dma((RB, 6)),
            dma((RB, 6)),
            dma((RB,)),
            dma((RB,)),
            dma((RB, 8)),
            dma((RB, 8)),
            dma((7,)),
            dma((7,)),
        ],
        compiler_params=pltpu.CompilerParams(
            collective_id=0, has_side_effects=True, vmem_limit_bytes=60 * 1024 * 1024
        ),
    )(
        three_center,
        coeffs.reshape(BLK_DEV, BS, OCC),
        sig_blocks,
        k_columns,
        slots,
    )


def solution(mesh):
    return jax.shard_map(
        per_device,
        mesh=mesh,
        in_specs=(
            P("aux", "rows", None, None, None),
            P("aux", None),
            P("rows", None),
            P("rows", None),
            P("rows", None),
        ),
        out_specs=P("rows", "aux", None),
        check_vma=False,
    )
```

time: 334 us -> 118 us (0.35)
  waiting for transfers between devices: 235 us -> 0 us
  Pallas kernels: 0 us -> 114 us
  local copies, waits for them, and re-layouts: 41.5 us -> 2.52 us
  matrix products: 26.4 us -> 0 us
  blocking collectives: 16.2 us -> 0 us
  between operations: 13.2 us -> 0.01 us
    all_gather x2 -> x0, waiting for transfers between devices: 166 us -> none  [the longest x1 125 us: per_device(): every_row = lax.all_gather(half, 'rows', axis=1, tiled=True)]
    pallas_call x0 -> x1, Pallas kernels: none -> 114 us  [per_device(): pl.pallas_call(kernel, out_shape=jax.ShapeDtypeStruct((8 * CAP, 8, BS), F...]
    reduce_scatter x1 -> x0, waiting for transfers between devices: 67.7 us -> none  [per_device(): lax.psum_scatter(partial_value, 'aux', scatter_dimension=1, tiled=True)]
    gather x6 -> x0, local copies, waits for them, and re-layouts: 28.9 us -> none  [the longest x5 25.6 us: per_device(): partners = jnp.take(every_row, k_columns[index], axis=1)]
    dot_general x6 -> x0, matrix products: 26.4 us -> none  [the longest x5 14.4 us: per_device(): jnp.einsum('pai,psbi->sab', half[:, index], partners, preferred_element_t...]
    all_to_all x1 -> x0, blocking collectives: 16.2 us -> none  [per_device(): lax.all_to_all(buffer, 'rows', split_axis=0, concat_axis=0, tiled=True)]
    concatenate x1 -> x0, local copies, waits for them, and re-layouts: 5.11 us -> none  [per_device(): partial_value = jnp.concatenate(pieces_list, axis=0)]
  transfers between devices with their start and end apart: 3 -> 0, of which waited for: 3 -> 0; matrix products, arithmetic and copies ran while one was open for 0% -> 0% of each run, Pallas kernels for 0% -> 0%
where the time goes in v1:
time: 118 us
  Pallas kernels  114 us (97%)
  local copies, waits for them, and re-layouts  2.52 us (2%)
  other arithmetic  1.67 us (1%)
    pallas_call x1, Pallas kernels, per_device(): pl.pallas_call(kernel, out_shape=jax.ShapeDtypeStruct((8 * CAP, 8, BS), F...  114 us

profile of v1, /device:TPU:0, one launch (start us, length us, event | category | flops | bytes accessed | tf_op | source)
XLA Modules:
  0.0 117.8 jit_solution(10243534456628242638)
XLA Ops:
  0.0 0.9 convert_reduce_fusion
  0.9 0.7 iota_add_fusion
  1.6 0.1 select_reduce_fusion
  1.7 0.7 reshape.21.slot_ref
  2.4 113.6 %shard_map.55 = f32[120,8,128]{2,1,0:T(8,128)} custom-call(bf16[8,5,16,128,128]{4,3,2,1,0:T(8,128)(2,1)} %t_hbm.1, bf16[8,128,128]{2,1,0:T(8,128)(2,1)} %bitcast.3, s32[5,16]{1,0:T(8,128)} %sig_ref.1, s32[5,12]{1,0:T(8,128)} %cols_ref.1, s32[8,15]{1,0:T(8,128)} %reshape.21.slot_ref), custom_call_target="tpu_custom_call" | custom-call | tf_op jit(solution)/shard_map/pallas_call | solution.py:316
  116.0 1.8 %copy.7 = f32[120,8,128]{2,1,0:T(8,128)} copy(f32[120,8,128]{2,1,0:T(8,128)} %shard_map.55) | data formatting | bytes 983040
